TPU v7x, 256 devices: a whole 4x4x8 slice. The times are simulated.
256 devices in a mesh: row: 32 (over x_lo, z, core), col: 8 (over y, x_hi).
Axes of the slice: x: 4 (x_hi: 2, x_lo: 2; x = x_hi * 2 + x_lo), y: 4, z: 8, core: 2. Of those that a mesh axis runs over, the one named last changes fastest.
Arguments:
- hessian: float32 [14336, 14336], P('row', 'col'), may hold values from -1 to 6, as said below
- dense_weight: float32 [14336, 1024], P('col', 'row'), may hold values from -6 to 6
- start_iterate: float32 [14336, 1024], P('col', 'row'), may hold values from -6 to 6
- start_multiplier: float32 [14336, 1024], P('col', 'row'), may hold values from -3 to 3
- keep_mask: int32 [14336, 1024], P('col', 'row'), may hold values 0 or 1
Outputs:
- iterate: float32 [14336, 1024], P('col', 'row')
- projected: float32 [14336, 1024], P('col', 'row')
- multiplier: float32 [14336, 1024], P('col', 'row')
Inputs may be any that keep to these rules, and one draw needn't show every extreme that they name: `hessian`: a calibration Hessian: symmetric up to rounding and positive definite.
All inputs are finite; a program needn't handle non-finite values. No bound on the sum of `keep_mask` on one device may be relied on, other than what follows from the above.
Results may differ from a plain program's by a relative error of at most 0.0001.
Values sent between devices are 32-bit elements; how exact they have to be, the bound alone decides.
A program may use at most 64 MiB of HBM per device.

v0:
```python
import jax
import jax.numpy as jnp
from jax import lax
from jax.sharding import PartitionSpec as P

ITERS = 2
step_size = 0.25
penalty = 1.0


def split_up(array, dim, length):
    before, after = (array.shape[:dim], array.shape[dim + 1 :])
    return jnp.moveaxis(array.reshape(*before, length, -1, *after), dim, 0)


def sum_at_owner(array, axis, dim):
    tiles = split_up(array, dim, lax.axis_size(axis))
    arrived = lax.all_to_all(tiles, axis, split_axis=0, concat_axis=0, tiled=True)
    return arrived.sum(axis=0)


def per_device(hessian, dense_weight, start_iterate, start_multiplier, keep_mask):
    keeping = keep_mask.astype(jnp.float32)
    iterate = start_iterate
    multiplier = start_multiplier
    projected = keeping * (iterate + multiplier)
    for rounds in range(ITERS):
        change = iterate - dense_weight
        gathered = lax.all_gather(change, "row", axis=1, tiled=True)
        partial_value = jnp.dot(
            hessian, gathered, precision=lax.Precision.HIGHEST, preferred_element_type=jnp.float32
        )
        summed = sum_at_owner(partial_value, "col", 0)
        shaped = summed.reshape(1, 1, summed.shape[0], summed.shape[1])
        relaid = lax.all_to_all(
            lax.all_to_all(shaped, "row", split_axis=3, concat_axis=0, tiled=True),
            "col",
            split_axis=0,
            concat_axis=1,
            tiled=True,
        )
        gradient = relaid.reshape(iterate.shape)
        iterate = iterate - step_size * (gradient + penalty * (iterate - projected + multiplier))
        projected = keeping * (iterate + multiplier)
        multiplier = multiplier + iterate - projected
    return (iterate, projected, multiplier)


def solution(mesh):
    return jax.shard_map(
        per_device,
        mesh=mesh,
        in_specs=(
            P("row", "col"),
            P("col", "row"),
            P("col", "row"),
            P("col", "row"),
            P("col", "row"),
        ),
        out_specs=(P("col", "row"), P("col", "row"), P("col", "row")),
        check_vma=False,
    )
```

profile of v0, /device:TPU:2, one launch (start us, length us, event | category | flops | bytes accessed | tf_op | source)
XLA Modules:
  0.0 363.2 jit_solution(16763132833857299460)
XLA Ops:
  7.2 0.0 copy-start
  7.2 0.0 all-gather.3.cloned.1.call-start
  7.2 1.9 sub.24
  9.1 0.0 all-gather.3.cloned.1.call-update
  9.2 0.0 all-gather.5.cloned.1.call-start
  9.2 75.1 %all-gather.3.cloned.1.call-done = f32[1792,1024]{0,1:T(8,128)} async-done(((f32[1792,32]{0,1:T(8,128)}), f32[1792,1024]{0,1:T(8,128)}) %all-gather.3.cloned.1.call-update) | async-done | bytes 7340048 | tf_op jit(solution)/shard_map/all_gather | solution.py:29
  84.3 0.0 copy-done
  84.3 12.9 %fusion.4 = f32[1024,448]{0,1:T(8,128)S(1)} fusion(f32[1792,1024]{0,1:T(8,128)} %all-gather.3.cloned.1.call-done, f32[448,1792]{1,0:T(8,128)S(1)} %copy-done), kind=kOutput, calls=%fused_computation.8 | convolution fusion | flops 9865003008 | bytes 12386304 | tf_op jit(solution)/shard_map/dot_general | solution.py:30
  97.2 31.7 %all_to_all.76 = f32[8,56,1024]{2,1,0:T(8,128)} all-to-all(f32[8,56,1024]{2,1,0:T(8,128)S(1)} %bitcast.54), channel_id=1, replica_groups=mesh['row'=32,'col'=8] {'col'}, dimensions={0} | all-to-all | bytes 3670016 | tf_op jit(solution)/shard_map/all_to_all | solution.py:18
  128.9 1.6 reduce_sum.18
  130.6 1.0 copy.10
  131.6 0.5 broadcast.8
  132.1 3.8 %reduce = f32[1024,56]{1,0:T(8,128)} reduce(f32[1024,1,1,56]{3,2,1,0:T(1,128)} %bitcast.48, f32[]{:T(128)} %broadcast.8), dimensions={1,2}, to_apply=%bitcast.36.reduce_sub_computation | reduce | bytes 458756
  135.9 0.0 copy-start.1
  135.9 2.3 reshape.32
  138.2 18.4 %all_to_all.77 = f32[32,1,1792]{2,1,0:T(1,128)} all-to-all(f32[32,1,1792]{2,1,0:T(1,128)} %reshape.32), channel_id=1, replica_groups=mesh['row'=32,'col'=8] {'row'}, dimensions={0} | all-to-all | bytes 458752 | tf_op jit(solution)/shard_map/all_to_all | solution.py:36
  156.6 2.8 reduce.1
  159.4 2.8 reshape.33
  162.2 2.3 reshape.34
  164.4 12.6 %all_to_all.78 = f32[8,1,7168]{2,1,0:T(1,128)} all-to-all(f32[8,1,7168]{2,1,0:T(1,128)} %reshape.34), channel_id=1, replica_groups=mesh['row'=32,'col'=8] {'col'}, dimensions={0} | all-to-all | bytes 458752 | tf_op jit(solution)/shard_map/all_to_all | solution.py:35
  177.1 2.8 reduce.2
  179.9 2.2 reshape.35
  182.1 2.2 copy.12
  184.2 2.0 reshape.28
  186.2 0.0 copy-done.1
  186.2 2.1 fusion.3
  188.4 0.0 all-gather.5.cloned.1.call-update
  188.4 64.4 %all-gather.5.cloned.1.call-done = f32[1792,1024]{0,1:T(8,128)} async-done(((f32[1792,32]{0,1:T(8,128)}), f32[1792,1024]{0,1:T(8,128)}) %all-gather.5.cloned.1.call-update) | async-done | bytes 7340048 | tf_op jit(solution)/shard_map/all_gather | solution.py:29
  252.8 12.9 %fusion.5 = f32[1024,448]{0,1:T(8,128)S(1)} fusion(f32[1792,1024]{0,1:T(8,128)} %all-gather.5.cloned.1.call-done, f32[448,1792]{1,0:T(8,128)S(1)} %copy-done), kind=kOutput, calls=%fused_computation.9 | convolution fusion | flops 9865003008 | bytes 12386304 | tf_op jit(solution)/shard_map/dot_general | solution.py:30
  265.7 31.7 %all_to_all.79 = f32[8,56,1024]{2,1,0:T(8,128)} all-to-all(f32[8,56,1024]{2,1,0:T(8,128)S(1)} %bitcast.55), channel_id=1, replica_groups=mesh['row'=32,'col'=8] {'col'}, dimensions={0} | all-to-all | bytes 3670016 | tf_op jit(solution)/shard_map/all_to_all | solution.py:18
  297.4 1.6 reduce_sum.19
  299.1 1.0 copy.13
  300.1 3.8 %reduce.3 = f32[1024,56]{1,0:T(8,128)} reduce(f32[1024,1,1,56]{3,2,1,0:T(1,128)} %bitcast.51, f32[]{:T(128)} %broadcast.8), dimensions={1,2}, to_apply=%bitcast.40.reduce_sub_computation | reduce | bytes 458756
  303.9 0.0 copy-start.2
  303.9 2.3 reshape.36
  306.2 18.4 %all_to_all.80 = f32[32,1,1792]{2,1,0:T(1,128)} all-to-all(f32[32,1,1792]{2,1,0:T(1,128)} %reshape.36), channel_id=1, replica_groups=mesh['row'=32,'col'=8] {'row'}, dimensions={0} | all-to-all | bytes 458752 | tf_op jit(solution)/shard_map/all_to_all | solution.py:36
  324.6 2.8 reduce.4
  327.4 2.8 reshape.37
  330.2 2.3 reshape.38
  332.4 12.6 %all_to_all.81 = f32[8,1,7168]{2,1,0:T(1,128)} all-to-all(f32[8,1,7168]{2,1,0:T(1,128)} %reshape.38), channel_id=1, replica_groups=mesh['row'=32,'col'=8] {'col'}, dimensions={0} | all-to-all | bytes 458752 | tf_op jit(solution)/shard_map/all_to_all | solution.py:35
  345.1 2.8 reduce.5
  347.9 2.2 reshape.39
  350.0 2.2 copy.15
  352.2 2.0 reshape.31
  354.2 0.0 copy-done.2
  354.2 2.1 fusion.2
Async XLA Ops:
  7.2 77.1 %copy-start = (f32[448,1792]{1,0:T(8,128)S(1)}, f32[448,1792]{1,0:T(8,128)}, u32[]{:S(2)}) copy-start(f32[448,1792]{1,0:T(8,128)} %param.5) | copy-start | bytes 9633796
  7.2 77.1 %all-gather.3.cloned.1.call-start = ((), (), s32[]{:S(2)}) async-start(), calls=%async_computation.6 | async-start | bytes 7569408 | tf_op jit(solution)/shard_map/all_gather | solution.py:29
  9.2 243.6 %all-gather.5.cloned.1.call-start = ((), (), s32[]{:S(2)}) async-start(), calls=%async_computation.7 | async-start | bytes 7569408 | tf_op jit(solution)/shard_map/all_gather | solution.py:29
  135.9 50.3 %copy-start.1 = (s32[1792,32]{0,1:T(8,128)S(1)}, s32[1792,32]{0,1:T(8,128)}, u32[]{:S(2)}) copy-start(s32[1792,32]{0,1:T(8,128)} %param.9) | copy-start | bytes 688132
  303.9 50.3 %copy-start.2 = (s32[1792,32]{0,1:T(8,128)S(1)}, s32[1792,32]{0,1:T(8,128)}, u32[]{:S(2)}) copy-start(s32[1792,32]{0,1:T(8,128)} %param.9) | copy-start | bytes 688132
Sparse Core Ops, SparseCore 0:
  10.4 73.8 all-gather.2
  188.5 64.2 all-gather.4
where the time goes:
time: 364 us; the launch traced here: 363 us
  waiting for transfers between devices  140 us (38%)
  blocking collectives  125 us (34%)
  local copies, waits for them, and re-layouts  29.9 us (8%)
  other arithmetic  28.2 us (8%)
  matrix products  25.8 us (7%)
  between operations  14.1 us (4%)
    all_gather x2, waiting for transfers between devices, per_device(): gathered = lax.all_gather(change, 'row', axis=1, tiled=True)  139 us
    all_to_all x2, blocking collectives, sum_at_owner(): lax.all_to_all(tiles, axis, split_axis=0, concat_axis=0, tiled=True)  63.5 us
    all_to_all x2, blocking collectives, per_device(): lax.all_to_all(shaped, 'row', split_axis=3, concat_axis=0, tiled=True)  36.8 us
    dot_general x2, matrix products, per_device(): jnp.dot(hessian, gathered, precision=lax.Precision.HIGHEST, preferred_ele...  25.8 us
    all_to_all x2, blocking collectives, per_device(): lax.all_to_all(lax.all_to_all(shaped, 'row', split_axis=3, concat_axis=0,...  25.3 us
    unnamed x15, local copies, waits for them, and re-layouts  19.6 us
    unnamed x2, other arithmetic  7.59 us
  transfers between devices with their start and end apart: 2, of which 2 were waited for; matrix products, arithmetic and copies ran while one was open for 0% of the time, Pallas kernels for 0%

commit v1 on v0

--- a/solution.py
+++ b/solution.py
@@ -26,7 +26,9 @@
     projected = keeping * (iterate + multiplier)
     for rounds in range(ITERS):
         change = iterate - dense_weight
-        gathered = lax.all_gather(change, "row", axis=1, tiled=True)
+        gathered = jnp.concatenate(
+            lax.all_to_all(jnp.stack([change] * lax.axis_size("row")), "row", 0, 0), axis=1
+        )
         partial_value = jnp.dot(
             hessian, gathered, precision=lax.Precision.HIGHEST, preferred_element_type=jnp.float32
         )

time: 364 us -> 548 us (1.51); the launches traced: 363 us -> 539 us
  blocking collectives: 125 us -> 458 us
  waiting for transfers between devices: 140 us -> 0 us
  between operations: 14.1 us -> 0.92 us
    all_to_all x0 -> x2, blocking collectives: none -> 339 us  [per_device(): lax.all_to_all(jnp.stack([change] * lax.axis_size('row')), 'row', 0, 0)]
    all_gather x2 -> x0, waiting for transfers between devices: 139 us -> none  [per_device(): gathered = lax.all_gather(change, 'row', axis=1, tiled=True)]
  transfers between devices with their start and end apart: 2 -> 0, of which waited for: 2 -> 0; matrix products, arithmetic and copies ran while one was open for 0% -> 0% of each run, Pallas kernels for 0% -> 0%
where the time goes in v1:
time: 548 us; the launch traced here: 539 us
  blocking collectives  458 us (84%)
  local copies, waits for them, and re-layouts  31.6 us (6%)
  other arithmetic  27.5 us (5%)
  matrix products  20.7 us (4%)
    all_to_all x2, blocking collectives, per_device(): lax.all_to_all(jnp.stack([change] * lax.axis_size('row')), 'row', 0, 0)  339 us
    all_to_all x2, blocking collectives, sum_at_owner(): lax.all_to_all(tiles, axis, split_axis=0, concat_axis=0, tiled=True)  60 us
    all_to_all x2, blocking collectives, per_device(): lax.all_to_all(shaped, 'row', split_axis=3, concat_axis=0, tiled=True)  33.9 us
    all_to_all x2, blocking collectives, per_device(): lax.all_to_all(lax.all_to_all(shaped, 'row', split_axis=3, concat_axis=0,...  25.3 us
    dot_general x2, matrix products, per_device(): jnp.dot(hessian, gathered, precision=lax.Precision.HIGHEST, preferred_ele...  20.7 us
    unnamed x15, local copies, waits for them, and re-layouts  19.6 us

profile of v1, /device:TPU:2, one launch (start us, length us, event | category | flops | bytes accessed | tf_op | source)
XLA Modules:
  0.0 538.5 jit_solution(16623669731851044670)
XLA Ops:
  0.6 0.0 copy-start
  0.6 1.2 sub.24
  1.9 0.8 stack.4
  2.7 172.1 %all_to_all.86 = f32[32,1792,32]{1,2,0:T(8,128)S(1)} all-to-all(f32[32,1792,32]{1,2,0:T(8,128)S(1)} %stack.4), channel_id=1, replica_groups=mesh['row'=32,'col'=8] {'row'}, dimensions={0} | all-to-all | bytes 14680064 | tf_op jit(solution)/shard_map/all_to_all | solution.py:30
  174.8 0.0 copy-done
  174.8 10.3 %fusion.4 = f32[1024,448]{0,1:T(8,128)S(1)} fusion(f32[1792,1024]{0,1:T(8,128)S(1)} %bitcast.54, f32[448,1792]{1,0:T(8,128)S(1)} %copy-done), kind=kOutput, calls=%fused_computation.8 | convolution fusion | flops 9865003008 | bytes 12386304 | tf_op jit(solution)/shard_map/dot_general | solution.py:32
  185.1 31.0 %all_to_all.87 = f32[8,56,1024]{2,1,0:T(8,128)} all-to-all(f32[8,56,1024]{2,1,0:T(8,128)S(1)} %bitcast.62), channel_id=1, replica_groups=mesh['row'=32,'col'=8] {'col'}, dimensions={0} | all-to-all | bytes 3670016 | tf_op jit(solution)/shard_map/all_to_all | solution.py:18
  216.1 1.6 reduce_sum.18
  217.8 1.0 copy.12
  218.8 0.5 broadcast.12
  219.3 3.8 reduce
  223.1 0.0 copy-start.1
  223.1 2.3 reshape.52
  225.4 17.1 %all_to_all.88 = f32[32,1,1792]{2,1,0:T(1,128)} all-to-all(f32[32,1,1792]{2,1,0:T(1,128)} %reshape.52), channel_id=1, replica_groups=mesh['row'=32,'col'=8] {'row'}, dimensions={0} | all-to-all | bytes 458752 | tf_op jit(solution)/shard_map/all_to_all | solution.py:38
  242.4 2.8 reduce.1
  245.3 2.8 reshape.53
  248.0 2.3 reshape.54
  250.3 12.6 %all_to_all.89 = f32[8,1,7168]{2,1,0:T(1,128)} all-to-all(f32[8,1,7168]{2,1,0:T(1,128)} %reshape.54), channel_id=1, replica_groups=mesh['row'=32,'col'=8] {'col'}, dimensions={0} | all-to-all | bytes 458752 | tf_op jit(solution)/shard_map/all_to_all | solution.py:37
  262.9 2.8 reduce.2
  265.7 2.2 reshape.55
  267.9 2.2 copy.14
  270.1 2.0 reshape.46
  272.1 0.0 copy-done.1
  272.1 2.0 fusion.3
  274.1 0.8 stack.5
  275.0 166.6 %all_to_all.90 = f32[32,1792,32]{1,2,0:T(8,128)S(1)} all-to-all(f32[32,1792,32]{1,2,0:T(8,128)S(1)} %stack.5), channel_id=1, replica_groups=mesh['row'=32,'col'=8] {'row'}, dimensions={0} | all-to-all | bytes 14680064 | tf_op jit(solution)/shard_map/all_to_all | solution.py:30
  441.6 10.3 %fusion.5 = f32[1024,448]{0,1:T(8,128)S(1)} fusion(f32[1792,1024]{0,1:T(8,128)S(1)} %bitcast.55, f32[448,1792]{1,0:T(8,128)S(1)} %copy-done), kind=kOutput, calls=%fused_computation.9 | convolution fusion | flops 9865003008 | bytes 12386304 | tf_op jit(solution)/shard_map/dot_general | solution.py:32
  452.0 29.0 %all_to_all.91 = f32[8,56,1024]{2,1,0:T(8,128)} all-to-all(f32[8,56,1024]{2,1,0:T(8,128)S(1)} %bitcast.63), channel_id=1, replica_groups=mesh['row'=32,'col'=8] {'col'}, dimensions={0} | all-to-all | bytes 3670016 | tf_op jit(solution)/shard_map/all_to_all | solution.py:18
  481.0 1.6 reduce_sum.19
  482.6 1.0 copy.15
  483.6 3.8 reduce.3
  487.4 0.0 copy-start.2
  487.4 2.3 reshape.56
  489.7 16.8 %all_to_all.92 = f32[32,1,1792]{2,1,0:T(1,128)} all-to-all(f32[32,1,1792]{2,1,0:T(1,128)} %reshape.56), channel_id=1, replica_groups=mesh['row'=32,'col'=8] {'row'}, dimensions={0} | all-to-all | bytes 458752 | tf_op jit(solution)/shard_map/all_to_all | solution.py:38
  506.6 2.8 reduce.4
  509.4 2.8 reshape.57
  512.2 2.3 reshape.58
  514.4 12.6 %all_to_all.93 = f32[8,1,7168]{2,1,0:T(1,128)} all-to-all(f32[8,1,7168]{2,1,0:T(1,128)} %reshape.58), channel_id=1, replica_groups=mesh['row'=32,'col'=8] {'col'}, dimensions={0} | all-to-all | bytes 458752 | tf_op jit(solution)/shard_map/all_to_all | solution.py:37
  527.0 2.8 reduce.5
  529.9 2.2 reshape.59
  532.0 2.2 copy.17
  534.2 2.0 reshape.51
  536.2 0.0 copy-done.2
  536.2 2.1 fusion.2
Async XLA Ops:
  0.6 174.2 %copy-start = (f32[448,1792]{1,0:T(8,128)S(1)}, f32[448,1792]{1,0:T(8,128)}, u32[]{:S(2)}) copy-start(f32[448,1792]{1,0:T(8,128)} %param.5) | copy-start | bytes 9633796
  223.1 49.0 %copy-start.1 = (s32[1792,32]{0,1:T(8,128)S(1)}, s32[1792,32]{0,1:T(8,128)}, u32[]{:S(2)}) copy-start(s32[1792,32]{0,1:T(8,128)} %param.9) | copy-start | bytes 688132
  487.4 48.8 %copy-start.2 = (s32[1792,32]{0,1:T(8,128)S(1)}, s32[1792,32]{0,1:T(8,128)}, u32[]{:S(2)}) copy-start(s32[1792,32]{0,1:T(8,128)} %param.9) | copy-start | bytes 688132
